TPU v7x, 32 devices: a whole 2x2x4 slice. The times are simulated.
32 devices in a mesh: dp: 2 (over core), row: 4 (over z), col: 4 (over y, x).
Axes of the slice: x: 2, y: 2, z: 4, core: 2. Of those that a mesh axis runs over, the one named last changes fastest.
Arguments:
- inputs: bfloat16 [16, 1024, 1024], P(('dp', 'row'), None, 'col'), may hold values from -6 to 6
- out_grad: bfloat16 [16, 1024, 1024], P(('dp', 'row'), None, 'col'), may hold values from -6 to 6
- seq_lengths: int32 [16], P(('dp', 'row')), may hold values from 1 to 1024, 12288 in all
- first_gain: bfloat16 [1024], replicated, may hold values from 0.099609375 to 1.8984375
- query_proj: bfloat16 [1024, 1024], P('row', 'col'), may hold values from -0.1875 to 0.1875
- key_proj: bfloat16 [1024, 1024], P('row', 'col'), may hold values from -0.1875 to 0.1875
- value_proj: bfloat16 [1024, 2048], P('row', 'col'), may hold values from -0.1875 to 0.1875
- decay_proj: bfloat16 [1024, 8], P('row', 'col'), may hold values from -0.1875 to 0.1875
- beta_proj: bfloat16 [1024, 8], P('row', 'col'), may hold values from -0.1875 to 0.1875
- gate_proj: bfloat16 [1024, 2048], P('row', 'col'), may hold values from -0.1875 to 0.1875
- query_conv: bfloat16 [4, 1024], P(None, 'col'), may hold values from -3 to 3
- key_conv: bfloat16 [4, 1024], P(None, 'col'), may hold values from -3 to 3
- value_conv: bfloat16 [4, 2048], P(None, 'col'), may hold values from -3 to 3
- decay_log: float32 [8], P('col'), may hold values from 0 to 2.77
- step_bias: float32 [8], P('col'), may hold values from -6.9 to -2.3
- output_gain: bfloat16 [256], replicated, may hold values from 0.099609375 to 1.8984375
- output_proj: bfloat16 [2048, 1024], P('col', 'row'), may hold values from -0.25 to 0.25
- second_gain: bfloat16 [1024], replicated, may hold values from 0.099609375 to 1.8984375
- hidden_gate: bfloat16 [1024, 2816], P('row', 'col'), may hold values from -0.1875 to 0.1875
- hidden_up: bfloat16 [1024, 2816], P('row', 'col'), may hold values from -0.1875 to 0.1875
- hidden_down: bfloat16 [2816, 1024], P('col', 'row'), may hold values from -0.109375 to 0.109375
Outputs:
- result: bfloat16 [16, 1024, 1024], P(('dp', 'row'), None, 'col')
- input_grad: float32 [16, 1024, 1024], P(('dp', 'row'), None, 'col')
- first_gain_grad: float32 [1024], P('col')
- query_proj_grad: float32 [1024, 1024], P('row', 'col')
- key_proj_grad: float32 [1024, 1024], P('row', 'col')
- value_proj_grad: float32 [1024, 2048], P('row', 'col')
- decay_proj_grad: float32 [1024, 8], P('row', 'col')
- beta_proj_grad: float32 [1024, 8], P('row', 'col')
- gate_proj_grad: float32 [1024, 2048], P('row', 'col')
- query_conv_grad: float32 [4, 1024], P(None, 'col')
- key_conv_grad: float32 [4, 1024], P(None, 'col')
- value_conv_grad: float32 [4, 2048], P(None, 'col')
- decay_log_grad: float32 [8], P('col')
- step_bias_grad: float32 [8], P('col')
- output_gain_grad: float32 [256], replicated
- output_proj_grad: float32 [2048, 1024], P('col', 'row')
- second_gain_grad: float32 [1024], P('col')
- hidden_gate_grad: float32 [1024, 2816], P('row', 'col')
- hidden_up_grad: float32 [1024, 2816], P('row', 'col')
- hidden_down_grad: float32 [2816, 1024], P('col', 'row')
Inputs may be any that keep to these rules, and one draw needn't show every extreme that they name: `seq_lengths`: the valid tokens of a sequence come first, the rest is padding; the longest sequence has exactly 1024.
All inputs are finite; a program needn't handle non-finite values. No bound on the sum of `seq_lengths` on one device may be relied on, other than what follows from the above.
Results may differ from a plain program's by a relative error of at most 0.014.
Values may be sent and summed in bfloat16 or wider, within the bound.
No kernel may reach another device: no remote copies, remote signals or barrier semaphores. Data moves between devices by JAX's collectives and lax.ppermute only.
A program may use at most 320 MiB of HBM per device.

v0:
```python
import jax
import jax.numpy as jnp
from jax import lax
from jax.sharding import PartitionSpec as P

D = 1024
DK = 128
DV = 256
CONV = 4
SPAN = 64
HIGHEST = lax.Precision.HIGHEST
NORM_EPS = 1e-05
UNIT_EPS = 1e-06


def causal_conv(values, kernel):
    length = values.shape[1]
    padded = jnp.pad(values, ((0, 0), (CONV - 1, 0), (0, 0)))
    summed = padded[:, 0:length] * kernel[0]
    for offset in range(1, CONV):
        summed = summed + padded[:, offset : offset + length] * kernel[offset]
    return jax.nn.silu(summed)


def unit_rows(values):
    return values * lax.rsqrt(jnp.sum(values * values, axis=-1, keepdims=True) + UNIT_EPS)


def delta_rule(queries, key_vecs, val_vecs, log_decay, beta_vals):
    seq_count, length, head_count = log_decay.shape
    blocks = length // SPAN

    def split_blocks(values):
        shaped = values.reshape((seq_count, blocks, SPAN, head_count) + values.shape[3:])
        return jnp.swapaxes(shaped, 2, 3)

    query_blk = split_blocks(queries)
    key_blk = split_blocks(key_vecs)
    value_blk = split_blocks(val_vecs)
    beta_blk = split_blocks(beta_vals)
    cumulative = jnp.cumsum(split_blocks(log_decay), axis=-1)
    log_gap = cumulative[..., :, None] - cumulative[..., None, :]
    row_ids = lax.broadcasted_iota(jnp.int32, (SPAN, SPAN), 0)
    col_ids = lax.broadcasted_iota(jnp.int32, (SPAN, SPAN), 1)
    lower_strict = row_ids > col_ids
    lower_incl = row_ids >= col_ids
    strict_fac = jnp.where(lower_strict, jnp.exp(jnp.where(lower_strict, log_gap, 0.0)), 0.0)
    incl_fac = jnp.where(lower_incl, jnp.exp(jnp.where(lower_incl, log_gap, 0.0)), 0.0)
    key_gram = jnp.einsum("sbhik,sbhjk->sbhij", key_blk, key_blk, precision=HIGHEST)
    coupling = beta_blk[..., None] * key_gram * strict_fac
    system = coupling + jnp.eye(SPAN, dtype=coupling.dtype)
    decayed = jnp.exp(cumulative)[..., None]
    right_side = jnp.concatenate(
        [beta_blk[..., None] * value_blk, beta_blk[..., None] * decayed * key_blk], axis=-1
    )
    solved = jax.scipy.linalg.solve_triangular(system, right_side, lower=True, unit_diagonal=True)
    value_dim = value_blk.shape[-1]
    new_vals = solved[..., :value_dim]
    key_part = solved[..., value_dim:]
    scores = jnp.einsum("sbhik,sbhjk->sbhij", query_blk, key_blk, precision=HIGHEST) * incl_fac
    query_dec = query_blk * decayed
    key_dec = key_blk * jnp.exp(cumulative[..., -1:] - cumulative)[..., None]
    block_decay = jnp.exp(cumulative[..., -1])[..., None, None]
    stacked = tuple(
        (
            jnp.moveaxis(piece, 1, 0)
            for piece in (new_vals, key_part, query_dec, scores, key_dec, block_decay)
        )
    )

    def advance(carry_state, pieces):
        new_part, key_piece, query_piece, score_piece, keydec_piece, decay_piece = pieces
        updates = new_part - jnp.einsum(
            "shck,shkv->shcv", key_piece, carry_state, precision=HIGHEST
        )
        output = jnp.einsum("shck,shkv->shcv", query_piece, carry_state, precision=HIGHEST)
        output = output + jnp.einsum("shij,shjv->shiv", score_piece, updates, precision=HIGHEST)
        carry_state = decay_piece * carry_state + jnp.einsum(
            "shck,shcv->shkv", keydec_piece, updates, precision=HIGHEST
        )
        return (carry_state, output)

    initial = jnp.zeros((seq_count, head_count, key_blk.shape[-1], value_dim), queries.dtype)
    unused_state, outputs = lax.scan(advance, initial, stacked)
    return jnp.transpose(outputs, (1, 0, 3, 2, 4)).reshape(seq_count, length, head_count, value_dim)


def mixer(
    query_in,
    key_in,
    value_in,
    decay_in,
    beta_in,
    gate_in,
    query_conv,
    key_conv,
    value_conv,
    decay_log,
    step_bias,
    output_gain,
):
    seq_count, length = (query_in.shape[0], query_in.shape[1])
    head_count = decay_log.shape[0]
    queries = unit_rows(
        causal_conv(query_in, query_conv).reshape(seq_count, length, head_count, DK)
    ) * DK ** (-0.5)
    key_vecs = unit_rows(causal_conv(key_in, key_conv).reshape(seq_count, length, head_count, DK))
    val_vecs = causal_conv(value_in, value_conv).reshape(seq_count, length, head_count, DV)
    beta_vals = jax.nn.sigmoid(beta_in)
    log_decay = -jnp.exp(decay_log) * jax.nn.softplus(decay_in + step_bias)
    mixer_out = delta_rule(queries, key_vecs, val_vecs, log_decay, beta_vals)
    normed = mixer_out * lax.rsqrt(
        jnp.mean(mixer_out * mixer_out, axis=-1, keepdims=True) + NORM_EPS
    )
    normed = normed * output_gain * jax.nn.silu(gate_in.reshape(seq_count, length, head_count, DV))
    return normed.reshape(seq_count, length, head_count * DV)


def gather_features(values):
    return lax.all_gather(values, "col", axis=1, tiled=True)


def sum_features(values):
    return lax.psum_scatter(values, "col", scatter_dimension=1, tiled=True)


def contract_rows(left, right):
    return lax.dot_general(
        left, right, (((0,), (0,)), ((), ())), preferred_element_type=jnp.float32
    )


def contract_cols(left, right):
    return lax.dot_general(
        left, right, (((1,), (1,)), ((), ())), preferred_element_type=jnp.float32
    )


def out_weight_grad(left, right):
    return lax.psum_scatter(
        contract_rows(left, right).astype(jnp.bfloat16), "row", scatter_dimension=1, tiled=True
    ).astype(jnp.float32)


def in_weight_grad(normed, grads):
    return lax.psum_scatter(
        contract_rows(normed, grads).astype(jnp.bfloat16), "row", scatter_dimension=0, tiled=True
    ).astype(jnp.float32)


def split_columns(values, widths):
    pieces = []
    offset = 0
    for column_width in widths:
        pieces.append(values[:, offset : offset + column_width])
        offset = offset + column_width
    return pieces


def on_device(
    inputs,
    out_grad,
    seq_lengths,
    first_gain,
    query_proj,
    key_proj,
    value_proj,
    decay_proj,
    beta_proj,
    gate_proj,
    query_conv,
    key_conv,
    value_conv,
    decay_log,
    step_bias,
    output_gain,
    output_proj,
    second_gain,
    hidden_gate,
    hidden_up,
    hidden_down,
):
    seq_count, length, col_width = inputs.shape
    tokens = seq_count * length
    col_index = lax.axis_index("col")
    gathered = (
        lax.all_gather(query_proj, "row", axis=0, tiled=True),
        lax.all_gather(key_proj, "row", axis=0, tiled=True),
        lax.all_gather(value_proj, "row", axis=0, tiled=True),
        lax.all_gather(decay_proj, "row", axis=0, tiled=True),
        lax.all_gather(beta_proj, "row", axis=0, tiled=True),
        lax.all_gather(gate_proj, "row", axis=0, tiled=True),
        lax.all_gather(hidden_gate, "row", axis=0, tiled=True),
        lax.all_gather(hidden_up, "row", axis=0, tiled=True),
        lax.all_gather(output_proj, "row", axis=1, tiled=True),
        lax.all_gather(hidden_down, "row", axis=1, tiled=True),
    )
    widths = [piece.shape[1] for piece in gathered[0:6]]
    input_weights = jnp.concatenate(gathered[0:6], axis=1)
    feed_weights = jnp.concatenate(gathered[6:8], axis=1)
    out_rows = gathered[8]
    down_rows = gathered[9]
    positions = lax.broadcasted_iota(jnp.int32, (seq_count, length), 1)
    valid_mask = (positions < seq_lengths[:, None]).astype(jnp.float32).reshape(tokens, 1)
    local_low = inputs.reshape(tokens, col_width)
    local_rows = local_low.astype(jnp.float32)
    full_rows = gather_features(local_low).astype(jnp.float32)
    first_scale = lax.rsqrt(jnp.mean(full_rows * full_rows, axis=1, keepdims=True) + NORM_EPS)
    first_full = first_gain.astype(jnp.float32)
    first_local = lax.dynamic_slice_in_dim(first_full, col_index * col_width, col_width)
    normed_first = (full_rows * first_scale * first_full * valid_mask).astype(jnp.bfloat16)
    projected = jnp.dot(normed_first, input_weights, preferred_element_type=jnp.float32)
    pieces = split_columns(projected, widths)
    mixer_args = tuple((piece.reshape(seq_count, length, piece.shape[1]) for piece in pieces)) + (
        query_conv.astype(jnp.float32),
        key_conv.astype(jnp.float32),
        value_conv.astype(jnp.float32),
        decay_log,
        step_bias,
        output_gain.astype(jnp.float32),
    )
    mixer_out, mixer_back = jax.vjp(mixer, *mixer_args)
    mixed_low = mixer_out.reshape(tokens, -1).astype(jnp.bfloat16)
    attention = sum_features(jnp.dot(mixed_low, out_rows, preferred_element_type=jnp.float32))
    hidden_res = local_rows + attention
    second_full = second_gain.astype(jnp.float32)
    second_local = lax.dynamic_slice_in_dim(second_full, col_index * col_width, col_width)
    full_res = lax.all_gather(hidden_res, "col", axis=1, tiled=True)
    second_scale = lax.rsqrt(jnp.mean(full_res * full_res, axis=1, keepdims=True) + NORM_EPS)
    normed_second = (full_res * second_scale * second_full * valid_mask).astype(jnp.bfloat16)
    gate_up = jnp.dot(normed_second, feed_weights, preferred_element_type=jnp.float32)
    ff_half = gate_up.shape[1] // 2
    gate_act = gate_up[:, :ff_half]
    up_act = gate_up[:, ff_half:]
    sigmoid_gate = jax.nn.sigmoid(gate_act)
    silu_gate = gate_act * sigmoid_gate
    hidden_act = (silu_gate * up_act).astype(jnp.bfloat16)
    feed_out = sum_features(jnp.dot(hidden_act, down_rows, preferred_element_type=jnp.float32))
    result = (
        ((hidden_res + feed_out) * valid_mask)
        .astype(jnp.bfloat16)
        .reshape(seq_count, length, col_width)
    )
    grad_out = out_grad.reshape(tokens, col_width).astype(jnp.float32) * valid_mask
    feed_grad_full = gather_features(grad_out.astype(jnp.bfloat16))
    down_grad = out_weight_grad(hidden_act, feed_grad_full)
    inner_grad = contract_cols(feed_grad_full, down_rows)
    gate_grad = (
        inner_grad * up_act * sigmoid_gate * (1.0 + gate_act * (1.0 - sigmoid_gate))
    ).astype(jnp.bfloat16)
    up_grad = (inner_grad * silu_gate).astype(jnp.bfloat16)
    gate_up_grad = jnp.concatenate([gate_grad, up_grad], axis=1)
    feed_weight_grad = in_weight_grad(normed_second, gate_up_grad)
    second_grad = sum_features(contract_cols(gate_up_grad, feed_weights)) * valid_mask
    second_hat = hidden_res * second_scale
    second_scaled = second_grad * second_local
    second_gain_grad = jnp.sum(second_grad * second_hat, axis=0)
    second_dot = lax.psum(jnp.sum(second_scaled * second_hat, axis=1, keepdims=True), "col")
    hidden_grad = grad_out + second_scale * (second_scaled - second_hat * second_dot / D)
    attn_grad_full = gather_features(hidden_grad.astype(jnp.bfloat16))
    out_proj_grad = out_weight_grad(mixed_low, attn_grad_full)
    mixed_grad = contract_cols(attn_grad_full, out_rows).reshape(seq_count, length, -1)
    mixer_grads = mixer_back(mixed_grad)
    proj_grad = jnp.concatenate(
        [grad_piece.reshape(tokens, -1) for grad_piece in mixer_grads[0:6]], axis=1
    ).astype(jnp.bfloat16)
    input_weight_grad = in_weight_grad(normed_first, proj_grad)
    first_grad = sum_features(contract_cols(proj_grad, input_weights)) * valid_mask
    first_hat = local_rows * first_scale
    first_scaled = first_grad * first_local
    first_gain_grad = jnp.sum(first_grad * first_hat, axis=0)
    first_dot, gain_out_grad = lax.psum(
        (jnp.sum(first_scaled * first_hat, axis=1, keepdims=True), mixer_grads[11]), "col"
    )
    input_grad = hidden_grad + first_scale * (first_scaled - first_hat * first_dot / D)
    input_weight_grad, out_proj_grad, feed_weight_grad, down_grad = (
        lax.psum(input_weight_grad.astype(jnp.bfloat16), "dp").astype(jnp.float32),
        lax.psum(out_proj_grad.astype(jnp.bfloat16), "dp").astype(jnp.float32),
        lax.psum(feed_weight_grad.astype(jnp.bfloat16), "dp").astype(jnp.float32),
        lax.psum(down_grad.astype(jnp.bfloat16), "dp").astype(jnp.float32),
    )
    small_sums = lax.psum(
        (
            first_gain_grad,
            second_gain_grad,
            mixer_grads[6],
            mixer_grads[7],
            mixer_grads[8],
            mixer_grads[9],
            mixer_grads[10],
            gain_out_grad,
        ),
        ("dp", "row"),
    )
    proj_grads = split_columns(input_weight_grad, widths)
    return (
        result,
        input_grad.reshape(seq_count, length, col_width),
        small_sums[0],
        proj_grads[0],
        proj_grads[1],
        proj_grads[2],
        proj_grads[3],
        proj_grads[4],
        proj_grads[5],
        small_sums[2],
        small_sums[3],
        small_sums[4],
        small_sums[5],
        small_sums[6],
        small_sums[7],
        out_proj_grad,
        small_sums[1],
        feed_weight_grad[:, :ff_half],
        feed_weight_grad[:, ff_half:],
        down_grad,
    )


def solution(mesh):
    in_specs = (
        P(("dp", "row"), None, "col"),
        P(("dp", "row"), None, "col"),
        P(("dp", "row")),
        P(),
        P("row", "col"),
        P("row", "col"),
        P("row", "col"),
        P("row", "col"),
        P("row", "col"),
        P("row", "col"),
        P(None, "col"),
        P(None, "col"),
        P(None, "col"),
        P("col"),
        P("col"),
        P(),
        P("col", "row"),
        P(),
        P("row", "col"),
        P("row", "col"),
        P("col", "row"),
    )
    out_specs = (
        P(("dp", "row"), None, "col"),
        P(("dp", "row"), None, "col"),
        P("col"),
        P("row", "col"),
        P("row", "col"),
        P("row", "col"),
        P("row", "col"),
        P("row", "col"),
        P("row", "col"),
        P(None, "col"),
        P(None, "col"),
        P(None, "col"),
        P("col"),
        P("col"),
        P(),
        P("col", "row"),
        P("col"),
        P("row", "col"),
        P("row", "col"),
        P("col", "row"),
    )
    return jax.shard_map(
        on_device, mesh=mesh, in_specs=in_specs, out_specs=out_specs, check_vma=False
    )
```

profile of v0, /device:TPU:1, one launch (start us, length us, event | category | flops | bytes accessed | tf_op | source)
XLA Modules:
  0.0 2145.6 jit_solution(803768090531166199)
XLA Ops:
  10.9 17.8 all_gather.43
  28.7 20.1 all_gather.44
  49.0 11.6 all_gather.46
  60.8 13.9 all_gather.47
  75.1 10.4 all-gather.15.cloned.1.call-done
  92.2 47.8 %all-gather.11.cloned.1.call-done = bf16[2048,1024]{1,0:T(8,128)(2,1)} async-done(((bf16[2048,256]{1,0:T(8,128)(2,1)}), bf16[2048,1024]{1,0:T(8,128)(2,1)}) %all-gather.11.cloned.1.call-update) | async-done | bytes 4194320 | tf_op jit(solution)/shard_map/all_gather | solution.py:120
  192.9 316.0 %custom-call.10 = f32[2,16,2,1,64,64]{4,5,3,2,1,0:T(8,128)} custom-call(f32[2,16,2,1,64,64]{5,4,3,2,1,0:T(8,128)} %fusion.109), custom_call_target="InvertDiagBlocksLowerTriangular" | custom-call | tf_op jit(solution)/shard_map/jvp(jit(_solve_triangular))/vmap(vmap(vmap()))/triangular_solve | solution.py:56
  516.5 10.2 fusion.90
  591.5 131.5 %while.44 = (s32[]{:T(128)}, f32[2,2,128,256]{3,2,1,0:T(8,128)S(1)}, f32[16,2,2,64,256]{4,2,3,0,1:T(2,128)}, f32[16,2,2,128,256]{4,3,2,1,0:T(8,128)}, f32[16,2,2...) while((s32[]{:T(128)}, ...), condition=%wide.region_5.6_spmd.clone, body=%wide.region_4.5_spmd.clone.sunk | while | flops 353239040 | bytes 6295230 | solution.py:84
  755.9 85.1 %reduce-scatter.9.cloned.1.call-done = f32[2048,256]{1,0:T(8,128)} async-done(((f32[2048,1024]{1,0:T(8,128)}), f32[2048,256]{1,0:T(8,128)}) %reduce-scatter.9.cloned.1.call-update) | async-done | bytes 2097168 | tf_op jit(solution)/shard_map/reduce_scatter | solution.py:124
  846.8 30.0 %all-gather.21.cloned.1.call-done = bf16[1024,704]{0,1:T(8,128)(2,1)} async-done(((bf16[256,704]{0,1:T(8,128)(2,1)}), bf16[1024,704]{0,1:T(8,128)(2,1)}) %all-gather.21.cloned.1.call-update) | async-done | bytes 1441808 | tf_op jit(solution)/shard_map/all_gather | solution.py:193
  879.4 32.9 %all-gather.23.cloned.1.call-done = bf16[1024,704]{0,1:T(8,128)(2,1)} async-done(((bf16[256,704]{0,1:T(8,128)(2,1)}), bf16[1024,704]{0,1:T(8,128)(2,1)}) %all-gather.23.cloned.1.call-update) | async-done | bytes 1441808 | tf_op jit(solution)/shard_map/all_gather | solution.py:194
  914.9 86.5 %all-gather.19.cloned.1.call-done = f32[2048,1024]{1,0:T(8,128)} async-done(((f32[2048,256]{1,0:T(8,128)}), f32[2048,1024]{1,0:T(8,128)}) %all-gather.19.cloned.1.call-update) | async-done | bytes 8388624 | tf_op jit(solution)/shard_map/all_gather | solution.py:228
  1007.1 11.3 fusion.217
  1018.4 18.8 all-gather.25.cloned.1.call-done
  1037.2 54.6 %all-gather.27.cloned.1.call-done = bf16[2048,1024]{1,0:T(8,128)(2,1)} async-done(((bf16[2048,256]{1,0:T(8,128)(2,1)}), bf16[2048,1024]{1,0:T(8,128)(2,1)}) %all-gather.27.cloned.1.call-update) | async-done | bytes 4194320 | tf_op jit(solution)/shard_map/all_gather | solution.py:120
  1091.8 11.3 multiply_convert_fusion.2
  1123.6 77.5 %reduce-scatter.13.cloned.1.call-done = f32[2048,256]{1,0:T(8,128)} async-done(((f32[2048,1024]{1,0:T(8,128)}), f32[2048,256]{1,0:T(8,128)}) %reduce-scatter.13.cloned.1.call-update) | async-done | bytes 2097168 | tf_op jit(solution)/shard_map/reduce_scatter | solution.py:124
  1210.9 79.5 %reduce-scatter.11.cloned.1.call-done = f32[2048,256]{1,0:T(8,128)} async-done(((f32[2048,1024]{1,0:T(8,128)}), f32[2048,256]{1,0:T(8,128)}) %reduce-scatter.11.cloned.1.call-update) | async-done | bytes 2097168 | tf_op jit(solution)/shard_map/reduce_scatter | solution.py:124
  1310.8 14.0 convolution_convert_fusion
  1324.8 22.5 %all-gather.29.cloned.1.call-done = bf16[2048,1024]{1,0:T(8,128)(2,1)} async-done(((bf16[2048,256]{1,0:T(8,128)(2,1)}), bf16[2048,1024]{1,0:T(8,128)(2,1)}) %all-gather.29.cloned.1.call-update) | async-done | bytes 4194320 | tf_op jit(solution)/shard_map/all_gather | solution.py:120
  1382.9 13.5 fusion.86
  1412.2 282.5 %while.45 = (s32[]{:T(128)}, f32[2,2,128,256]{3,2,1,0:T(8,128)S(1)}, f32[16,2,2,64,256]{4,3,2,1,0:T(8,128)}, f32[16,2,2,64,128]{4,3,2,1,0:T(8,128)S(1)}, f32[16,...) while((s32[]{:T(128)}, ...), condition=%wide.region_16.17_spmd.clone, body=%wide.region_14.16_spmd.clone.sunk | while | flops 706019328 | bytes 9969441 | solution.py:84
  1703.1 12.2 fusion.72
  1771.7 11.3 multiply_reduce_fusion.3
  1878.0 27.9 %concatenate.20 = bf16[2048,1540]{0,1:T(8,128)(2,1)} concatenate(bf16[2048,256]{0,1:T(8,128)(2,1)} %copy.480, bf16[2048,256]{0,1:T(8,128)(2,1)S(1)} %copy.481, bf16[2048,512]{0,1:T(8,128)(2,1)} %copy.482, bf16[2048,2]{0,1:T(2,128)(2,1)S(1)} %fusion.200, bf16[2048,2]{0,1:T(2,128)(2,1)S(1)} %fusion.193, bf16[2048,512]{0,1:T(8,128)(2,1)S(1)} %copy-done.30), dimensions={1} | concatenate | bytes 12615680 | tf_op jit(solution)/shard_map/concatenate | solution.py:264
  1905.9 11.8 convolution_convert_fusion.1
  1917.9 60.7 %reduce-scatter.17.cloned.1.call-done = bf16[256,1540]{0,1:T(8,128)(2,1)} async-done(((bf16[1024,1540]{0,1:T(8,128)(2,1)}), bf16[256,1540]{0,1:T(8,128)(2,1)}) %reduce-scatter.17.cloned.1.call-update) | async-done | bytes 788496 | tf_op jit(solution)/shard_map/reduce_scatter | solution.py:146
  1978.6 12.0 fusion.236
  1991.6 11.4 all-reduce.36.cloned.1.call-done
  2012.7 80.9 %reduce-scatter.15.cloned.1.call-done = f32[2048,256]{1,0:T(8,128)} async-done(((f32[2048,1024]{1,0:T(8,128)}), f32[2048,256]{1,0:T(8,128)}) %reduce-scatter.15.cloned.1.call-update) | async-done | bytes 2097168 | tf_op jit(solution)/shard_map/reduce_scatter | solution.py:124
  2103.3 32.2 %all-reduce.31 = (f32[256]{0:T(256)}, f32[4,256]{1,0:T(4,128)}, f32[4,256]{1,0:T(4,128)}, f32[4,512]{1,0:T(4,128)}, f32[2]{0:T(128)}, /*index=5*/f32[2]{0:T(128)}, f32[256]{0:T(256)}, f32[256]{0:T(256)}) all-reduce(f32[256]{0:T(256)S(1)} %get-tuple-element.741, ...), channel_id=1, replica_groups=mesh['dp'=2,'row'=4,'col'=4] {'dp','row'}, use_global_device_ids=true, to_apply=%region_32.33 | all-reduce | flops 4868 | bytes 38944 | tf_op jit(solution)/shard_map/psum | solution.py:282
  (806 shorter events, 881.9 us)
Async XLA Ops:
  7.3 67.8 %all-gather.13.cloned.1.call-start = ((), (), s32[]{:S(2)}) async-start(), calls=%async_computation.9 | async-start | bytes 1310720 | tf_op jit(solution)/shard_map/all_gather | solution.py:189
  8.0 77.5 %all-gather.15.cloned.1.call-start = ((), (), s32[]{:S(2)}) async-start(), calls=%async_computation.10 | async-start | bytes 1310720 | tf_op jit(solution)/shard_map/all_gather | solution.py:192
  8.8 131.2 %all-gather.11.cloned.1.call-start = ((), (), s32[]{:S(2)}) async-start(), calls=%async_computation.8 | async-start | bytes 5242880 | tf_op jit(solution)/shard_map/all_gather | solution.py:120
  9.5 737.4 %all-gather.17.cloned.1.call-start = ((), (), s32[]{:S(2)}) async-start(), calls=%async_computation.11 | async-start | bytes 1310720 | tf_op jit(solution)/shard_map/all_gather | solution.py:195
  10.1 830.9 %reduce-scatter.9.cloned.1.call-start = ((), (), s32[]{:S(2)}) async-start(), calls=%async_computation.12 | async-start | bytes 10485760 | tf_op jit(solution)/shard_map/reduce_scatter | solution.py:124
  10.2 572.0 %copy-start.68 = (pred[64,64]{1,0:T(8,128)(4,1)}, pred[64,64]{1,0:T(8,128)(4,1)S(1)}, u32[]{:S(2)}) copy-start(pred[64,64]{1,0:T(8,128)(4,1)S(1)} %iota_compare_fusion) | copy-start | bytes 12292
  10.9 1299.8 %copy-start.59 = (f32[1,8,2,128]{3,1,2,0:T(8,128)}, f32[1,8,2,128]{3,1,2,0:T(8,128)S(1)}, u32[]{:S(2)}) copy-start(f32[1,8,2,128]{3,1,2,0:T(8,128)S(1)} %copy.661) | copy-start | bytes 24580
  74.9 441.6 %copy-start.80 = (f32[1,512]{1,0:T(1,128)}, f32[1,512]{1,0:T(1,128)S(1)}, u32[]{:S(2)}) copy-start(f32[1,512]{1,0:T(1,128)S(1)} %get-tuple-element.878) | copy-start | bytes 6148
  74.9 441.5 %copy-start.82 = (f32[1,512]{1,0:T(1,128)}, f32[1,512]{1,0:T(1,128)S(1)}, u32[]{:S(2)}) copy-start(f32[1,512]{1,0:T(1,128)S(1)} %get-tuple-element.879) | copy-start | bytes 6148
  74.9 441.5 %copy-start.84 = (f32[1,512]{1,0:T(1,128)}, f32[1,512]{1,0:T(1,128)S(1)}, u32[]{:S(2)}) copy-start(f32[1,512]{1,0:T(1,128)S(1)} %get-tuple-element.880) | copy-start | bytes 6148
  74.9 441.5 %copy-start.86 = (f32[1,512]{1,0:T(1,128)}, f32[1,512]{1,0:T(1,128)S(1)}, u32[]{:S(2)}) copy-start(f32[1,512]{1,0:T(1,128)S(1)} %get-tuple-element.881) | copy-start | bytes 6148
  75.0 475.5 %copy-start.89 = (f32[1,256]{1,0:T(1,128)}, f32[1,256]{1,0:T(1,128)S(1)}, u32[]{:S(2)}) copy-start(f32[1,256]{1,0:T(1,128)S(1)} %get-tuple-element.882) | copy-start | bytes 3076
  75.0 475.5 %copy-start.91 = (f32[1,256]{1,0:T(1,128)}, f32[1,256]{1,0:T(1,128)S(1)}, u32[]{:S(2)}) copy-start(f32[1,256]{1,0:T(1,128)S(1)} %get-tuple-element.883) | copy-start | bytes 3076
  75.0 475.4 %copy-start.93 = (f32[1,256]{1,0:T(1,128)}, f32[1,256]{1,0:T(1,128)S(1)}, u32[]{:S(2)}) copy-start(f32[1,256]{1,0:T(1,128)S(1)} %get-tuple-element.884) | copy-start | bytes 3076
  75.0 475.4 %copy-start.95 = (f32[1,256]{1,0:T(1,128)}, f32[1,256]{1,0:T(1,128)S(1)}, u32[]{:S(2)}) copy-start(f32[1,256]{1,0:T(1,128)S(1)} %get-tuple-element.885) | copy-start | bytes 3076
  171.5 410.7 %copy-start = (f32[2,16,64,2,128]{4,3,2,1,0:T(2,128)}, f32[2,16,64,2,128]{4,3,2,1,0:T(2,128)S(1)}, u32[]{:S(2)}) copy-start(f32[2,16,64,2,128]{4,3,2,1,0:T(2,128)S(1)} %reshape.417) | copy-start | bytes 6291460
  182.7 399.4 %copy-start.43 = (f32[2,16,64,2]{2,3,1,0:T(2,128)}, f32[2,16,64,2]{2,3,1,0:T(2,128)S(1)}, u32[]{:S(2)}) copy-start(f32[2,16,64,2]{2,3,1,0:T(2,128)S(1)} %copy.377) | copy-start | bytes 49156
  184.5 391.4 %copy-start.37 = (f32[2,16,2,64]{3,1,2,0:T(8,128)}, f32[2,16,2,64]{3,1,2,0:T(8,128)S(1)}, u32[]{:S(2)}) copy-start(f32[2,16,2,64]{3,1,2,0:T(8,128)S(1)} %reduce_window_sum.24) | copy-start | bytes 49156
  754.5 122.3 %all-gather.21.cloned.1.call-start = ((), (), s32[]{:S(2)}) async-start(), calls=%async_computation.14 | async-start | bytes 1802240 | tf_op jit(solution)/shard_map/all_gather | solution.py:193
  755.1 157.2 %all-gather.23.cloned.1.call-start = ((), (), s32[]{:S(2)}) async-start(), calls=%async_computation.15 | async-start | bytes 1802240 | tf_op jit(solution)/shard_map/all_gather | solution.py:194
  755.9 245.5 %all-gather.19.cloned.1.call-start = ((), (), s32[]{:S(2)}) async-start(), calls=%async_computation.13 | async-start | bytes 10485760 | tf_op jit(solution)/shard_map/all_gather | solution.py:228
  844.2 193.0 %all-gather.25.cloned.1.call-start = ((), (), s32[]{:S(2)}) async-start(), calls=%async_computation.16 | async-start | bytes 1802240 | tf_op jit(solution)/shard_map/all_gather | solution.py:196
  844.9 246.9 %all-gather.27.cloned.1.call-start = ((), (), s32[]{:S(2)}) async-start(), calls=%async_computation.18 | async-start | bytes 5242880 | tf_op jit(solution)/shard_map/all_gather | solution.py:120
  846.7 354.3 %reduce-scatter.13.cloned.1.call-start = ((), (), s32[]{:S(2)}) async-start(), calls=%async_computation.19 | async-start | bytes 10485760 | tf_op jit(solution)/shard_map/reduce_scatter | solution.py:124
  1114.6 175.9 %reduce-scatter.11.cloned.1.call-start = ((), (), s32[]{:S(2)}) async-start(), calls=%async_computation.17 | async-start | bytes 10485760 | tf_op jit(solution)/shard_map/reduce_scatter | solution.py:124
  1123.5 223.8 %all-gather.29.cloned.1.call-start = ((), (), s32[]{:S(2)}) async-start(), calls=%async_computation.20 | async-start | bytes 5242880 | tf_op jit(solution)/shard_map/all_gather | solution.py:120
  1294.6 623.2 %reduce-scatter.23.cloned.1.call-start = ((), (), s32[]{:S(2)}) async-start(), calls=%async_computation.25 | async-start | bytes 1802240 | tf_op jit(solution)/shard_map/reduce_scatter | solution.py:140
  1302.2 615.7 %reduce-scatter.21.cloned.1.call-start = ((), (), s32[]{:S(2)}) async-start(), calls=%async_computation.24 | async-start | bytes 3604480 | tf_op jit(solution)/shard_map/reduce_scatter | solution.py:146
  1324.7 593.1 %reduce-scatter.19.cloned.1.call-start = ((), (), s32[]{:S(2)}) async-start(), calls=%async_computation.23 | async-start | bytes 1310720 | tf_op jit(solution)/shard_map/reduce_scatter | solution.py:140
  1877.8 100.7 %reduce-scatter.17.cloned.1.call-start = ((), (), s32[]{:S(2)}) async-start(), calls=%async_computation.22 | async-start | bytes 3952640 | tf_op jit(solution)/shard_map/reduce_scatter | solution.py:146
  1917.8 85.3 %all-reduce.36.cloned.1.call-start = ((), (), s32[]{:S(2)}) async-start(), calls=%async_computation.26 | async-start | bytes 4268032 | tf_op jit(solution)/shard_map/psum | solution.py:277
  1978.6 115.1 %reduce-scatter.15.cloned.1.call-start = ((), (), s32[]{:S(2)}) async-start(), calls=%async_computation.21 | async-start | bytes 10485760 | tf_op jit(solution)/shard_map/reduce_scatter | solution.py:124
  (116 other events, 2757.5 us)
Sparse Core Ops, SparseCore 0:
  9.7 41.9 all-gather.12
  53.2 32.2 all-gather.14
  87.4 52.5 all-gather.10
  141.4 28.8 all-gather.16
  754.7 86.3 reduce-scatter.8
  842.5 34.2 all-gather.20
  878.4 33.7 all-gather.22
  914.2 87.0 all-gather.18
  1003.0 34.2 all-gather.24
  1039.6 52.1 all-gather.26
  1114.7 86.3 reduce-scatter.12
  1204.0 86.4 reduce-scatter.10
  1294.7 52.5 all-gather.28
  1349.6 33.0 reduce-scatter.22
  1385.0 55.0 reduce-scatter.20
  1878.0 27.0 reduce-scatter.18
  1917.9 60.6 reduce-scatter.16
  1981.0 22.0 all-reduce.35
  2006.4 87.1 reduce-scatter.14
where the time goes:
time: 2160 us; the launch traced here: 2150 us
  waiting for transfers between devices  703 us (33%)
  matrix products  522 us (24%)
  other arithmetic  512 us (24%)
  local copies, waits for them, and re-layouts  280 us (13%)
  blocking collectives  110 us (5%)
    reduce_scatter x4, waiting for transfers between devices, sum_features(): return lax.psum_scatter(values, 'col', scatter_dimension=1, tiled=True)  323 us
    another operation x3, other arithmetic, delta_rule(): jax.scipy.linalg.solve_triangular(system, right_side, lower=True, unit_di...  318 us
    all_gather x3, waiting for transfers between devices, gather_features(): return lax.all_gather(values, 'col', axis=1, tiled=True)  125 us
    dot_general x48, matrix products, advance(): jnp.einsum('shck,shkv->shcv', key_piece, carry_state, precision=HIGHEST)  86.5 us
    all_gather x1, waiting for transfers between devices, on_device(): full_res = lax.all_gather(hidden_res, 'col', axis=1, tiled=True)  86.5 us
    dot_general x48, matrix products, advance(): jnp.einsum('shij,shjv->shiv', score_piece, updates, precision=HIGHEST)  84.7 us
    dot_general x48, matrix products, advance(): jnp.einsum('shck,shkv->shcv', query_piece, carry_state, precision=HIGHEST)  83.7 us
    dot_general x48, matrix products, advance(): jnp.einsum('shck,shcv->shkv', keydec_piece, updates, precision=HIGHEST)  83.3 us
  transfers between devices with their start and end apart: 19, of which 14 were waited for; matrix products, arithmetic and copies ran while one was open for 58% of the time, Pallas kernels for 0%

commit v1 on v0

--- a/solution.py
+++ b/solution.py
@@ -11,6 +11,27 @@
 HIGHEST = lax.Precision.HIGHEST
 NORM_EPS = 1e-05
 UNIT_EPS = 1e-06
+
+
+def ring_gather(value, axis, dim):
+    devices, index, extent = (lax.axis_size(axis), lax.axis_index(axis), value.shape[dim])
+    right = [(i, (i + 1) % devices) for i in range(devices)]
+    downward = [(i, (i - 1) % devices) for i in range(devices)]
+    whole = jnp.zeros((*value.shape[:dim], devices * extent, *value.shape[dim + 1 :]), value.dtype)
+    whole = lax.dynamic_update_slice_in_dim(whole, value, index * extent, axis=dim)
+    from_left = from_right = value
+    middle = devices // 2
+    for hop in range(1, middle + 1):
+        from_left = lax.ppermute(from_left, axis, right)
+        whole = lax.dynamic_update_slice_in_dim(
+            whole, from_left, (index - hop) % devices * extent, axis=dim
+        )
+        if hop < devices - middle:
+            from_right = lax.ppermute(from_right, axis, downward)
+            whole = lax.dynamic_update_slice_in_dim(
+                whole, from_right, (index + hop) % devices * extent, axis=dim
+            )
+    return whole
 
 
 def causal_conv(values, kernel):
@@ -117,7 +138,7 @@
 
 
 def gather_features(values):
-    return lax.all_gather(values, "col", axis=1, tiled=True)
+    return ring_gather(values, "col", 1)
 
 
 def sum_features(values):

time: 2160 us -> 2100 us (0.972)
  waiting for transfers between devices: 703 us -> 599 us
  local copies, waits for them, and re-layouts: 280 us -> 306 us
    all_gather x3 -> x0, waiting for transfers between devices: 125 us -> none  [gather_features(): return lax.all_gather(values, 'col', axis=1, tiled=True)]
    ppermute x0 -> x9, waiting for transfers between devices: none -> 107 us  [the longest x6 80.2 us: ring_gather(): from_left = lax.ppermute(from_left, axis, right)]
    all_gather x1, waiting for transfers between devices: 32.9 us -> 0.01 us  [on_device(): lax.all_gather(hidden_up, 'row', axis=0, tiled=True)]
    all_gather x1, waiting for transfers between devices: 30 us -> 0.01 us  [on_device(): lax.all_gather(hidden_gate, 'row', axis=0, tiled=True)]
  transfers between devices with their start and end apart: 19 -> 25, of which waited for: 14 -> 15; matrix products, arithmetic and copies ran while one was open for 58% -> 62% of each run, Pallas kernels for 0% -> 0%
where the time goes in v1:
time: 2100 us; the launch traced here: 2080 us
  waiting for transfers between devices  599 us (29%)
  matrix products  522 us (25%)
  other arithmetic  514 us (24%)
  local copies, waits for them, and re-layouts  306 us (15%)
  blocking collectives  111 us (5%)
    reduce_scatter x4, waiting for transfers between devices, sum_features(): return lax.psum_scatter(values, 'col', scatter_dimension=1, tiled=True)  323 us
    another operation x3, other arithmetic, delta_rule(): jax.scipy.linalg.solve_triangular(system, right_side, lower=True, unit_di...  318 us
    dot_general x48, matrix products, advance(): jnp.einsum('shck,shkv->shcv', key_piece, carry_state, precision=HIGHEST)  86.4 us
    dot_general x48, matrix products, advance(): jnp.einsum('shij,shjv->shiv', score_piece, updates, precision=HIGHEST)  84.8 us
    dot_general x48, matrix products, advance(): jnp.einsum('shck,shkv->shcv', query_piece, carry_state, precision=HIGHEST)  83.8 us
    dot_general x48, matrix products, advance(): jnp.einsum('shck,shcv->shkv', keydec_piece, updates, precision=HIGHEST)  83.4 us
    ppermute x6, waiting for transfers between devices, ring_gather(): from_left = lax.ppermute(from_left, axis, right)  80.2 us
    all_gather x1, waiting for transfers between devices, on_device(): full_res = lax.all_gather(hidden_res, 'col', axis=1, tiled=True)  74.7 us
  transfers between devices with their start and end apart: 25, of which 15 were waited for; matrix products, arithmetic and copies ran while one was open for 62% of the time, Pallas kernels for 0%

profile of v1, /device:TPU:1, one launch (start us, length us, event | category | flops | bytes accessed | tf_op | source)
XLA Modules:
  0.0 2079.5 jit_solution(4208248263146705623)
XLA Ops:
  12.7 16.5 all_gather.33
  29.2 20.8 %all_gather.34 = bf16[1024,256]{1,0:T(8,128)(2,1)S(1)} all-gather(bf16[256,256]{1,0:T(8,128)(2,1)} %param.30), channel_id=1, replica_groups=mesh['dp'=2,'row'=4,'col'=4] {'row'}, dimensions={0}, use_global_device_ids=true | all-gather | bytes 655360 | tf_op jit(solution)/shard_map/all_gather | solution.py:209
  51.0 12.4 all_gather.36
  63.4 14.8 all_gather.37
  99.8 9.4 fusion.213
  169.0 316.0 %custom-call.10 = f32[2,16,2,1,64,64]{4,5,3,2,1,0:T(8,128)} custom-call(f32[2,16,2,1,64,64]{5,4,3,2,1,0:T(8,128)} %fusion.109), custom_call_target="InvertDiagBlocksLowerTriangular" | custom-call | tf_op jit(solution)/shard_map/jvp(jit(_solve_triangular))/vmap(vmap(vmap()))/triangular_solve | solution.py:77
  490.4 10.2 fusion.90
  547.5 130.9 %while.44 = (s32[]{:T(128)}, f32[2,2,128,256]{3,2,1,0:T(8,128)S(1)}, f32[16,2,2,64,256]{4,2,3,0,1:T(2,128)}, f32[16,2,2,128,256]{4,3,2,1,0:T(8,128)}, f32[16,2,2...) while((s32[]{:T(128)}, ...), condition=%wide.region_5.6_spmd.clone, body=%wide.region_4.5_spmd.clone.sunk | while | flops 353239040 | bytes 6295230 | solution.py:105
  711.1 95.3 %reduce-scatter.9.cloned.1.call-done = f32[2048,256]{1,0:T(8,128)} async-done(((f32[2048,1024]{1,0:T(8,128)}), f32[2048,256]{1,0:T(8,128)}) %reduce-scatter.9.cloned.1.call-update) | async-done | bytes 2097168 | tf_op jit(solution)/shard_map/reduce_scatter | solution.py:145
  816.3 22.7 %collective-permute-done.3 = bf16[2048,256]{1,0:T(8,128)(2,1)S(1)} collective-permute-done((bf16[2048,256]{1,0:T(8,128)(2,1)}, bf16[2048,256]{1,0:T(8,128)(2,1)S(1)}, u32[]{:S(2)}, u32[]{:S(2)}) %collective-permute-start.3) | collective-permute-done | bytes 1048608 | tf_op jit(solution)/shard_map/ppermute | solution.py:25
  840.5 21.1 %collective-permute-done.4 = bf16[2048,256]{1,0:T(8,128)(2,1)S(1)} collective-permute-done((bf16[2048,256]{1,0:T(8,128)(2,1)}, bf16[2048,256]{1,0:T(8,128)(2,1)S(1)}, u32[]{:S(2)}, u32[]{:S(2)}) %collective-permute-start.4) | collective-permute-done | bytes 1048608 | tf_op jit(solution)/shard_map/ppermute | solution.py:30
  862.7 21.4 %collective-permute-done.5 = bf16[2048,256]{1,0:T(8,128)(2,1)} collective-permute-done((bf16[2048,256]{1,0:T(8,128)(2,1)S(1)}, bf16[2048,256]{1,0:T(8,128)(2,1)}, u32[]{:S(2)}, u32[]{:S(2)}) %collective-permute-start.5) | collective-permute-done | bytes 1048608 | tf_op jit(solution)/shard_map/ppermute | solution.py:25
  891.9 74.7 %all-gather.14.cloned.1.call-done = f32[2048,1024]{1,0:T(8,128)} async-done(((f32[2048,256]{1,0:T(8,128)}), f32[2048,1024]{1,0:T(8,128)}) %all-gather.14.cloned.1.call-update) | async-done | bytes 8388624 | tf_op jit(solution)/shard_map/all_gather | solution.py:249
  972.4 11.3 fusion.217
  983.7 18.8 all-gather.20.cloned.1.call-done
  1002.5 11.3 multiply_convert_fusion.2
  1042.1 69.2 %reduce-scatter.13.cloned.1.call-done = f32[2048,256]{1,0:T(8,128)} async-done(((f32[2048,1024]{1,0:T(8,128)}), f32[2048,256]{1,0:T(8,128)}) %reduce-scatter.13.cloned.1.call-update) | async-done | bytes 2097168 | tf_op jit(solution)/shard_map/reduce_scatter | solution.py:145
  1121.2 79.5 %reduce-scatter.11.cloned.1.call-done = f32[2048,256]{1,0:T(8,128)} async-done(((f32[2048,1024]{1,0:T(8,128)}), f32[2048,256]{1,0:T(8,128)}) %reduce-scatter.11.cloned.1.call-update) | async-done | bytes 2097168 | tf_op jit(solution)/shard_map/reduce_scatter | solution.py:145
  1219.6 14.3 collective-permute-done.6
  1234.5 14.0 convolution_convert_fusion
  1258.7 20.1 collective-permute-done.8
  1315.2 13.5 fusion.86
  1344.5 282.8 %while.45 = (s32[]{:T(128)}, f32[2,2,128,256]{3,2,1,0:T(8,128)S(1)}, f32[16,2,2,64,256]{4,3,2,1,0:T(8,128)}, f32[16,2,2,64,128]{4,3,2,1,0:T(8,128)S(1)}, f32[16,...) while((s32[]{:T(128)}, ...), condition=%wide.region_16.17_spmd.clone, body=%wide.region_14.16_spmd.clone.sunk | while | flops 706019328 | bytes 9969441 | solution.py:105
  1635.8 12.2 fusion.72
  1704.6 11.2 multiply_reduce_fusion.3
  1811.4 28.0 %concatenate.20 = bf16[2048,1540]{0,1:T(8,128)(2,1)} concatenate(bf16[2048,256]{0,1:T(8,128)(2,1)} %copy.480, bf16[2048,256]{0,1:T(8,128)(2,1)S(1)} %copy.481, bf16[2048,512]{0,1:T(8,128)(2,1)} %copy.482, bf16[2048,2]{0,1:T(2,128)(2,1)S(1)} %fusion.200, bf16[2048,2]{0,1:T(2,128)(2,1)S(1)} %fusion.193, bf16[2048,512]{0,1:T(8,128)(2,1)S(1)} %copy-done.30), dimensions={1} | concatenate | bytes 12615680 | tf_op jit(solution)/shard_map/concatenate | solution.py:285
  1839.4 11.8 convolution_convert_fusion.1
  1851.3 61.4 %reduce-scatter.17.cloned.1.call-done = bf16[256,1540]{0,1:T(8,128)(2,1)} async-done(((bf16[1024,1540]{0,1:T(8,128)(2,1)}), bf16[256,1540]{0,1:T(8,128)(2,1)}) %reduce-scatter.17.cloned.1.call-update) | async-done | bytes 788496 | tf_op jit(solution)/shard_map/reduce_scatter | solution.py:167
  1912.8 11.9 fusion.234
  1925.7 11.5 all-reduce.36.cloned.1.call-done
  1948.7 78.9 %reduce-scatter.15.cloned.1.call-done = f32[2048,256]{1,0:T(8,128)} async-done(((f32[2048,1024]{1,0:T(8,128)}), f32[2048,256]{1,0:T(8,128)}) %reduce-scatter.15.cloned.1.call-update) | async-done | bytes 2097168 | tf_op jit(solution)/shard_map/reduce_scatter | solution.py:145
  2037.1 32.2 %all-reduce.31 = (f32[256]{0:T(256)}, f32[4,256]{1,0:T(4,128)}, f32[4,256]{1,0:T(4,128)}, f32[4,512]{1,0:T(4,128)}, f32[2]{0:T(128)}, /*index=5*/f32[2]{0:T(128)}, f32[256]{0:T(256)}, f32[256]{0:T(256)}) all-reduce(f32[256]{0:T(256)S(1)} %get-tuple-element.741, ...), channel_id=1, replica_groups=mesh['dp'=2,'row'=4,'col'=4] {'dp','row'}, use_global_device_ids=true, to_apply=%region_32.33 | all-reduce | flops 4868 | bytes 38944 | tf_op jit(solution)/shard_map/psum | solution.py:303
  (829 shorter events, 915.4 us)
Async XLA Ops:
  7.3 78.5 %all-gather.10.cloned.1.call-start = ((), (), s32[]{:S(2)}) async-start(), calls=%async_computation.9 | async-start | bytes 1310720 | tf_op jit(solution)/shard_map/all_gather | solution.py:213
  8.0 77.8 %all-gather.8.cloned.1.call-start = ((), (), s32[]{:S(2)}) async-start(), calls=%async_computation.8 | async-start | bytes 1310720 | tf_op jit(solution)/shard_map/all_gather | solution.py:210
  8.8 693.6 %all-gather.12.cloned.1.call-start = ((), (), s32[]{:S(2)}) async-start(), calls=%async_computation.10 | async-start | bytes 1310720 | tf_op jit(solution)/shard_map/all_gather | solution.py:216
  8.8 69.6 %collective-permute-start = (bf16[2048,256]{1,0:T(8,128)(2,1)}, bf16[2048,256]{1,0:T(8,128)(2,1)S(1)}, u32[]{:S(2)}, u32[]{:S(2)}) collective-permute-start(bf16[2048,256]{1,0:T(8,128)(2,1)} %bitcast.445), channel_id=1, source_target_pairs={{0,1},{1,2},{2,3},{3,0},{4,5},{5,6},{6,7},{7,4},{8,9},{9,10},{10,1... | collective-permute-start | bytes 3145736 | tf_op jit(solution)/shard_map/ppermute | solution.py:25
  10.9 72.6 %collective-permute-start.1 = (bf16[2048,256]{1,0:T(8,128)(2,1)}, bf16[2048,256]{1,0:T(8,128)(2,1)}, u32[]{:S(2)}, u32[]{:S(2)}) collective-permute-start(bf16[2048,256]{1,0:T(8,128)(2,1)} %bitcast.446), channel_id=1, source_target_pairs={{0,3},{1,0},{2,1},{3,2},{4,7},{5,4},{6,5},{7,6},{8,11},{9,8},{10,9... | collective-permute-start | bytes 3145736 | tf_op jit(solution)/shard_map/ppermute | solution.py:30
  11.9 794.5 %reduce-scatter.9.cloned.1.call-start = ((), (), s32[]{:S(2)}) async-start(), calls=%async_computation.11 | async-start | bytes 10485760 | tf_op jit(solution)/shard_map/reduce_scatter | solution.py:145
  50.1 487.9 %copy-start.69 = (pred[64,64]{1,0:T(8,128)(4,1)}, pred[64,64]{1,0:T(8,128)(4,1)S(1)}, u32[]{:S(2)}) copy-start(pred[64,64]{1,0:T(8,128)(4,1)S(1)} %iota_compare_fusion) | copy-start | bytes 12292
  50.6 1183.8 %copy-start.57 = (f32[1,8,2,128]{3,1,2,0:T(8,128)}, f32[1,8,2,128]{3,1,2,0:T(8,128)S(1)}, u32[]{:S(2)}) copy-start(f32[1,8,2,128]{3,1,2,0:T(8,128)S(1)} %copy.661) | copy-start | bytes 24580
  78.3 412.0 %copy-start.80 = (f32[1,512]{1,0:T(1,128)}, f32[1,512]{1,0:T(1,128)S(1)}, u32[]{:S(2)}) copy-start(f32[1,512]{1,0:T(1,128)S(1)} %get-tuple-element.879) | copy-start | bytes 6148
  78.3 412.0 %copy-start.82 = (f32[1,512]{1,0:T(1,128)}, f32[1,512]{1,0:T(1,128)S(1)}, u32[]{:S(2)}) copy-start(f32[1,512]{1,0:T(1,128)S(1)} %get-tuple-element.880) | copy-start | bytes 6148
  78.4 412.0 %copy-start.84 = (f32[1,512]{1,0:T(1,128)}, f32[1,512]{1,0:T(1,128)S(1)}, u32[]{:S(2)}) copy-start(f32[1,512]{1,0:T(1,128)S(1)} %get-tuple-element.881) | copy-start | bytes 6148
  78.4 412.0 %copy-start.86 = (f32[1,512]{1,0:T(1,128)}, f32[1,512]{1,0:T(1,128)S(1)}, u32[]{:S(2)}) copy-start(f32[1,512]{1,0:T(1,128)S(1)} %get-tuple-element.882) | copy-start | bytes 6148
  78.4 15.7 collective-permute-start.2
  127.1 410.9 %copy-start = (f32[2,16,64,2,128]{4,3,2,1,0:T(2,128)}, f32[2,16,64,2,128]{4,3,2,1,0:T(2,128)S(1)}, u32[]{:S(2)}) copy-start(f32[2,16,64,2,128]{4,3,2,1,0:T(2,128)S(1)} %reshape.417) | copy-start | bytes 6291460
  709.9 176.5 %all-gather.16.cloned.1.call-start = ((), (), s32[]{:S(2)}) async-start(), calls=%async_computation.13 | async-start | bytes 1802240 | tf_op jit(solution)/shard_map/all_gather | solution.py:214
  710.5 178.8 %all-gather.18.cloned.1.call-start = ((), (), s32[]{:S(2)}) async-start(), calls=%async_computation.14 | async-start | bytes 1802240 | tf_op jit(solution)/shard_map/all_gather | solution.py:215
  711.1 255.5 %all-gather.14.cloned.1.call-start = ((), (), s32[]{:S(2)}) async-start(), calls=%async_computation.12 | async-start | bytes 10485760 | tf_op jit(solution)/shard_map/all_gather | solution.py:249
  809.6 192.9 %all-gather.20.cloned.1.call-start = ((), (), s32[]{:S(2)}) async-start(), calls=%async_computation.15 | async-start | bytes 1802240 | tf_op jit(solution)/shard_map/all_gather | solution.py:217
  813.9 25.1 %collective-permute-start.3 = (bf16[2048,256]{1,0:T(8,128)(2,1)}, bf16[2048,256]{1,0:T(8,128)(2,1)S(1)}, u32[]{:S(2)}, u32[]{:S(2)}) collective-permute-start(bf16[2048,256]{1,0:T(8,128)(2,1)} %get-tuple-element.894), channel_id=1, source_target_pairs={{0,1},{1,2},{2,3},{3,0},{4,5},{5,6},{6,7},{7,4},{8,9},{9,10},{10,1... | collective-permute-start | bytes 3145736 | tf_op jit(solution)/shard_map/ppermute | solution.py:25
  815.0 46.6 %collective-permute-start.4 = (bf16[2048,256]{1,0:T(8,128)(2,1)}, bf16[2048,256]{1,0:T(8,128)(2,1)S(1)}, u32[]{:S(2)}, u32[]{:S(2)}) collective-permute-start(bf16[2048,256]{1,0:T(8,128)(2,1)} %get-tuple-element.894), channel_id=1, source_target_pairs={{0,3},{1,0},{2,1},{3,2},{4,7},{5,4},{6,5},{7,6},{8,11},{9,8},{10,9... | collective-permute-start | bytes 3145736 | tf_op jit(solution)/shard_map/ppermute | solution.py:30
  839.0 45.0 %collective-permute-start.5 = (bf16[2048,256]{1,0:T(8,128)(2,1)S(1)}, bf16[2048,256]{1,0:T(8,128)(2,1)}, u32[]{:S(2)}, u32[]{:S(2)}) collective-permute-start(bf16[2048,256]{1,0:T(8,128)(2,1)S(1)} %collective-permute-done.3), channel_id=1, source_target_pairs={{0,1},{1,2},{2,3},{3,0},{4,5},{5,6},{6,7},{7,4},{8,9},{9,10},{10,1... | collective-permute-start | bytes 3145736 | tf_op jit(solution)/shard_map/ppermute | solution.py:25
  839.3 272.0 %reduce-scatter.13.cloned.1.call-start = ((), (), s32[]{:S(2)}) async-start(), calls=%async_computation.17 | async-start | bytes 10485760 | tf_op jit(solution)/shard_map/reduce_scatter | solution.py:145
  1025.2 175.4 %reduce-scatter.11.cloned.1.call-start = ((), (), s32[]{:S(2)}) async-start(), calls=%async_computation.16 | async-start | bytes 10485760 | tf_op jit(solution)/shard_map/reduce_scatter | solution.py:145
  1034.2 817.0 %reduce-scatter.23.cloned.1.call-start = ((), (), s32[]{:S(2)}) async-start(), calls=%async_computation.22 | async-start | bytes 1802240 | tf_op jit(solution)/shard_map/reduce_scatter | solution.py:161
  1042.1 809.2 %reduce-scatter.21.cloned.1.call-start = ((), (), s32[]{:S(2)}) async-start(), calls=%async_computation.21 | async-start | bytes 3604480 | tf_op jit(solution)/shard_map/reduce_scatter | solution.py:167
  1208.7 25.2 %collective-permute-start.6 = (bf16[2048,256]{1,0:T(8,128)(2,1)}, bf16[2048,256]{1,0:T(8,128)(2,1)}, u32[]{:S(2)}, u32[]{:S(2)}) collective-permute-start(bf16[2048,256]{1,0:T(8,128)(2,1)} %get-tuple-element.828), channel_id=1, source_target_pairs={{0,1},{1,2},{2,3},{3,0},{4,5},{5,6},{6,7},{7,4},{8,9},{9,10},{10,1... | collective-permute-start | bytes 3145736 | tf_op jit(solution)/shard_map/ppermute | solution.py:25
  1218.3 38.0 %collective-permute-start.7 = (bf16[2048,256]{1,0:T(8,128)(2,1)}, bf16[2048,256]{1,0:T(8,128)(2,1)}, u32[]{:S(2)}, u32[]{:S(2)}) collective-permute-start(bf16[2048,256]{1,0:T(8,128)(2,1)} %get-tuple-element.828), channel_id=1, source_target_pairs={{0,3},{1,0},{2,1},{3,2},{4,7},{5,4},{6,5},{7,6},{8,11},{9,8},{10,9... | collective-permute-start | bytes 3145736 | tf_op jit(solution)/shard_map/ppermute | solution.py:30
  1233.9 44.9 %collective-permute-start.8 = (bf16[2048,256]{1,0:T(8,128)(2,1)}, bf16[2048,256]{1,0:T(8,128)(2,1)S(1)}, u32[]{:S(2)}, u32[]{:S(2)}) collective-permute-start(bf16[2048,256]{1,0:T(8,128)(2,1)} %collective-permute-done.6), channel_id=1, source_target_pairs={{0,1},{1,2},{2,3},{3,0},{4,5},{5,6},{6,7},{7,4},{8,9},{9,10},{10,1... | collective-permute-start | bytes 3145736 | tf_op jit(solution)/shard_map/ppermute | solution.py:25
  1248.5 602.8 %reduce-scatter.19.cloned.1.call-start = ((), (), s32[]{:S(2)}) async-start(), calls=%async_computation.20 | async-start | bytes 1310720 | tf_op jit(solution)/shard_map/reduce_scatter | solution.py:161
  1811.3 101.4 %reduce-scatter.17.cloned.1.call-start = ((), (), s32[]{:S(2)}) async-start(), calls=%async_computation.19 | async-start | bytes 3952640 | tf_op jit(solution)/shard_map/reduce_scatter | solution.py:167
  1851.2 86.0 %all-reduce.36.cloned.1.call-start = ((), (), s32[]{:S(2)}) async-start(), calls=%async_computation.23 | async-start | bytes 4268032 | tf_op jit(solution)/shard_map/psum | solution.py:298
  1912.7 114.9 %reduce-scatter.15.cloned.1.call-start = ((), (), s32[]{:S(2)}) async-start(), calls=%async_computation.18 | async-start | bytes 10485760 | tf_op jit(solution)/shard_map/reduce_scatter | solution.py:145
  (122 other events, 3837.0 us)
Sparse Core Ops, SparseCore 0:
  9.7 41.8 all-gather.9
  53.1 32.0 all-gather.7
  86.8 29.2 all-gather.11
  710.1 96.3 reduce-scatter.8
  807.9 34.2 all-gather.15
  843.7 33.7 all-gather.17
  879.5 87.0 all-gather.13
  968.2 34.2 all-gather.19
  1025.4 85.9 reduce-scatter.12
  1114.2 86.3 reduce-scatter.10
  1203.1 33.1 reduce-scatter.22
  1248.6 59.3 reduce-scatter.20
  1811.4 27.8 reduce-scatter.18
  1851.3 61.3 reduce-scatter.16
  1915.1 22.0 all-reduce.35
  1940.4 87.1 reduce-scatter.14
